TPU v7x, 512 devices: a whole 4x4x16 slice. The times are simulated.
512 devices in a mesh: doc: 16 (over y_lo, x, core), blk: 32 (over y_hi, z).
Axes of the slice: x: 4, y: 4 (y_hi: 2, y_lo: 2; y = y_hi * 2 + y_lo), z: 16, core: 2. Of those that a mesh axis runs over, the one named last changes fastest.
Arguments:
- query_rows: bfloat16 [256, 98304], P('blk', 'doc'), may hold values from -6 to 6
- row_values: bfloat16 [16, 32, 32, 128, 256], P('doc', 'blk'), may hold values from -0.25 to 0.25
- row_slots: int32 [16, 32, 32, 128], P('doc', 'blk'), may hold values from 0 to 49151, as said below
- row_counts: int32 [16, 32, 32], P('doc', 'blk'), may hold values from 16 to 128, as said below
Outputs:
- gram: float32 [256, 65536], P('doc', 'blk')
Inputs may be any that keep to these rules, and one draw needn't show every extreme that they name: row_slots[d, s, o, j] = (s * 192 + e) * 8 + b for a document e of source s's 192 and a feature block b of owner o; the 128 entries of one (d, s, o) are distinct. Slots j >= row_counts[d, s, o] carry no data; for every d some owner receives 128 rows from every source.
All inputs are finite; a program needn't handle non-finite values.
Results may differ from a plain program's by a relative error of at most 0.0003.
Values may be sent and summed in bfloat16 or wider, within the bound.
No kernel may reach another device: no remote copies, remote signals or barrier semaphores. Data moves between devices by JAX's collectives and lax.ppermute only.
A program may use at most 192 MiB of HBM per device.

v0:
```python
import jax
import jax.numpy as jnp
from jax import lax
from jax.sharding import PartitionSpec as P

F = 65536
BW = 256


def per_device(query_rows, row_values, row_slots, row_counts):
    owners = lax.axis_size("blk")
    doc_count = query_rows.shape[1]
    own_width = F // owners
    per_owner = own_width // BW
    places = row_slots.shape[3]
    live_slot = jnp.arange(places, dtype=jnp.int32)[None, None, None, :] < row_counts[:, :, :, None]
    targets = jnp.where(live_slot, row_slots, doc_count * per_owner)
    got_values, got_targets = (
        lax.all_to_all(row_values, "blk", split_axis=2, concat_axis=2, tiled=True),
        lax.all_to_all(targets, "blk", split_axis=2, concat_axis=2, tiled=True),
    )
    flat_values = got_values.reshape(-1, BW)
    flat_targets = got_targets.reshape(-1)
    live_rows = flat_targets < doc_count * per_owner
    doc_of = jnp.where(live_rows, flat_targets // per_owner, doc_count).astype(jnp.int32)
    block_of = flat_targets % per_owner
    block_ids = jnp.arange(per_owner, dtype=jnp.int32)
    gathered = lax.all_gather(query_rows, "blk", axis=0, tiled=True)
    safe_doc = jnp.minimum(doc_of, doc_count - 1)
    picked_queries = jnp.take(gathered, safe_doc, axis=1)

    def block_tile(block):
        keep = (live_rows & (block_of == block))[:, None]
        masked = jnp.where(keep, flat_values, jnp.zeros_like(flat_values))
        return jnp.dot(picked_queries, masked, preferred_element_type=jnp.float32)

    tiles = lax.map(block_tile, block_ids)
    partial_value = tiles.transpose(1, 0, 2).reshape(gathered.shape[0], own_width)
    return lax.psum_scatter(partial_value, "doc", scatter_dimension=0, tiled=True)


def solution(mesh):
    in_specs = (
        P("blk", "doc"),
        P("doc", "blk", None, None, None),
        P("doc", "blk", None, None),
        P("doc", "blk", None),
    )
    out_specs = P("doc", "blk")
    return jax.shard_map(
        per_device, mesh=mesh, in_specs=in_specs, out_specs=out_specs, check_vma=False
    )
```

profile of v0, /device:TPU:32, one launch (start us, length us, event | category | flops | bytes accessed | tf_op | source)
XLA Modules:
  0.0 378.6 jit_solution(15423100263397606264)
XLA Ops:
  6.5 0.8 compare_select_fusion.2
  7.4 31.3 %all_to_all.10 = s32[1,1,32,128]{3,1,0,2:T(1,128)S(1)} all-to-all(s32[1,1,32,128]{3,1,0,2:T(1,128)S(1)} %compare_select_fusion.2), channel_id=1, replica_groups=mesh['doc'=16,'blk'=32] {'blk'}, dimensions={2} | all-to-all | bytes 32768 | tf_op jit(solution)/shard_map/all_to_all | solution.py:20
  38.7 5.9 %all-to-all-start.1 = ((bf16[1,1,32,128,256]{4,3,1,0,2:T(8,128)(2,1)}), bf16[1,1,32,128,256]{4,3,1,0,2:T(8,128)(2,1)}, u32[]{:S(2)}, u32[]{:S(2)}) async-start(bf16[1,1,32,128,256]{4,3,1,0,2:T(8,128)(2,1)} %bitcast.35), calls=%async_computation.1 | async-start | bytes 4194304 | tf_op jit(solution)/shard_map/all_to_all | solution.py:19
  44.6 0.0 all-gather.2.cloned.1.call-start
  44.6 0.7 all-gather.2.cloned.1.call-update
  45.3 0.0 reduce-scatter.2.cloned.1.call-start
  45.4 0.1 compare_select_fusion
  45.5 187.5 %all-gather.2.cloned.1.call-done = bf16[256,6144]{1,0:T(8,128)(2,1)} async-done(((bf16[8,6144]{1,0:T(8,128)(2,1)}), bf16[256,6144]{1,0:T(8,128)(2,1)}) %all-gather.2.cloned.1.call-update) | async-done | bytes 3145744 | tf_op jit(solution)/shard_map/all_gather | solution.py:28
  233.0 3.2 copy.10
  236.2 16.9 %gather_fusion = bf16[4096,256]{1,0:T(8,128)(2,1)} fusion(bf16[256,6144]{0,1:T(8,128)(2,1)S(1)} %copy.10, s32[4096]{0:T(1024)S(1)} %broadcast_clamp_fusion), kind=kCustom, calls=%fused_computation | custom fusion | bytes 4210688 | tf_op jit(solution)/shard_map/jit(_take)/gather | solution.py:30
  253.1 1.9 select_bitcast_fusion
  255.1 2.9 copy.11
  258.0 0.0 all-to-all-done.1
  258.0 45.3 %while.10 = (s32[]{:T(128)}, f32[8,256,256]{1,2,0:T(8,128)}, s32[8]{0:T(128)S(1)}, s32[4096]{0:T(1024)S(1)}, pred[4096]{0:T(1024)(128)(4,1)S(1)}, /*index=5*/bf1...) while((s32[]{:T(128)}, f32[8,256,256]{1,2,0:T(8,128)}, s32[8]{0:T(128)S(1)}, s32[4096]{0:T(1024)S(1)}, ...), condition=%wide.region_1.2_spmd, body=%wide.region_0.1_spmd.sunk | while | flops 537927680 | bytes 4485733 | solution.py:37
  258.0 0.7 dynamic_slice.5
  258.7 0.7 compare_and_fusion.3
  259.4 4.3 %fusion.21 = f32[8,256,256]{1,2,0:T(8,128)} fusion(f32[8,256,256]{1,2,0:T(8,128)} %get-tuple-element.125, s32[]{:T(128)} %get-tuple-element.124, bf16[256,4096]{1,0:T(8,128)(2,1)} %get-tuple-element.138, bf16[4096,256]{1,0:T(8,128)(2,1)} %get-tuple-element.137, pred[4096]{0:T(1024)(128)(4,1)S(1)} %compare_and_fusion.3), kind=kOutput, calls=%fused_computation.5.clone.1 | convolution fusion | flops 537919488 | bytes 4461056 | tf_op jit(solution)/shard_map/while/body/eval_jaxpr/dot_general | solution.py:35
  263.7 0.6 dynamic_slice.5
  264.3 0.7 compare_and_fusion.3
  265.0 4.3 %fusion.21 = f32[8,256,256]{1,2,0:T(8,128)} fusion(f32[8,256,256]{1,2,0:T(8,128)} %get-tuple-element.125, s32[]{:T(128)} %get-tuple-element.124, bf16[256,4096]{1,0:T(8,128)(2,1)} %get-tuple-element.138, bf16[4096,256]{1,0:T(8,128)(2,1)} %get-tuple-element.137, pred[4096]{0:T(1024)(128)(4,1)S(1)} %compare_and_fusion.3), kind=kOutput, calls=%fused_computation.5.clone.1 | convolution fusion | flops 537919488 | bytes 4461056 | tf_op jit(solution)/shard_map/while/body/eval_jaxpr/dot_general | solution.py:35
  269.4 0.6 dynamic_slice.5
  270.0 0.7 compare_and_fusion.3
  270.7 4.3 %fusion.21 = f32[8,256,256]{1,2,0:T(8,128)} fusion(f32[8,256,256]{1,2,0:T(8,128)} %get-tuple-element.125, s32[]{:T(128)} %get-tuple-element.124, bf16[256,4096]{1,0:T(8,128)(2,1)} %get-tuple-element.138, bf16[4096,256]{1,0:T(8,128)(2,1)} %get-tuple-element.137, pred[4096]{0:T(1024)(128)(4,1)S(1)} %compare_and_fusion.3), kind=kOutput, calls=%fused_computation.5.clone.1 | convolution fusion | flops 537919488 | bytes 4461056 | tf_op jit(solution)/shard_map/while/body/eval_jaxpr/dot_general | solution.py:35
  275.0 0.6 dynamic_slice.5
  275.7 0.7 compare_and_fusion.3
  276.4 4.3 %fusion.21 = f32[8,256,256]{1,2,0:T(8,128)} fusion(f32[8,256,256]{1,2,0:T(8,128)} %get-tuple-element.125, s32[]{:T(128)} %get-tuple-element.124, bf16[256,4096]{1,0:T(8,128)(2,1)} %get-tuple-element.138, bf16[4096,256]{1,0:T(8,128)(2,1)} %get-tuple-element.137, pred[4096]{0:T(1024)(128)(4,1)S(1)} %compare_and_fusion.3), kind=kOutput, calls=%fused_computation.5.clone.1 | convolution fusion | flops 537919488 | bytes 4461056 | tf_op jit(solution)/shard_map/while/body/eval_jaxpr/dot_general | solution.py:35
  280.7 0.6 dynamic_slice.5
  281.3 0.7 compare_and_fusion.3
  282.0 4.3 %fusion.21 = f32[8,256,256]{1,2,0:T(8,128)} fusion(f32[8,256,256]{1,2,0:T(8,128)} %get-tuple-element.125, s32[]{:T(128)} %get-tuple-element.124, bf16[256,4096]{1,0:T(8,128)(2,1)} %get-tuple-element.138, bf16[4096,256]{1,0:T(8,128)(2,1)} %get-tuple-element.137, pred[4096]{0:T(1024)(128)(4,1)S(1)} %compare_and_fusion.3), kind=kOutput, calls=%fused_computation.5.clone.1 | convolution fusion | flops 537919488 | bytes 4461056 | tf_op jit(solution)/shard_map/while/body/eval_jaxpr/dot_general | solution.py:35
  286.3 0.6 dynamic_slice.5
  287.0 0.7 compare_and_fusion.3
  287.7 4.3 %fusion.21 = f32[8,256,256]{1,2,0:T(8,128)} fusion(f32[8,256,256]{1,2,0:T(8,128)} %get-tuple-element.125, s32[]{:T(128)} %get-tuple-element.124, bf16[256,4096]{1,0:T(8,128)(2,1)} %get-tuple-element.138, bf16[4096,256]{1,0:T(8,128)(2,1)} %get-tuple-element.137, pred[4096]{0:T(1024)(128)(4,1)S(1)} %compare_and_fusion.3), kind=kOutput, calls=%fused_computation.5.clone.1 | convolution fusion | flops 537919488 | bytes 4461056 | tf_op jit(solution)/shard_map/while/body/eval_jaxpr/dot_general | solution.py:35
  292.0 0.6 dynamic_slice.5
  292.6 0.7 compare_and_fusion.3
  293.3 4.3 %fusion.21 = f32[8,256,256]{1,2,0:T(8,128)} fusion(f32[8,256,256]{1,2,0:T(8,128)} %get-tuple-element.125, s32[]{:T(128)} %get-tuple-element.124, bf16[256,4096]{1,0:T(8,128)(2,1)} %get-tuple-element.138, bf16[4096,256]{1,0:T(8,128)(2,1)} %get-tuple-element.137, pred[4096]{0:T(1024)(128)(4,1)S(1)} %compare_and_fusion.3), kind=kOutput, calls=%fused_computation.5.clone.1 | convolution fusion | flops 537919488 | bytes 4461056 | tf_op jit(solution)/shard_map/while/body/eval_jaxpr/dot_general | solution.py:35
  297.7 0.6 dynamic_slice.5
  298.3 0.7 compare_and_fusion.3
  299.0 4.3 %fusion.21 = f32[8,256,256]{1,2,0:T(8,128)} fusion(f32[8,256,256]{1,2,0:T(8,128)} %get-tuple-element.125, s32[]{:T(128)} %get-tuple-element.124, bf16[256,4096]{1,0:T(8,128)(2,1)} %get-tuple-element.138, bf16[4096,256]{1,0:T(8,128)(2,1)} %get-tuple-element.137, pred[4096]{0:T(1024)(128)(4,1)S(1)} %compare_and_fusion.3), kind=kOutput, calls=%fused_computation.5.clone.1 | convolution fusion | flops 537919488 | bytes 4461056 | tf_op jit(solution)/shard_map/while/body/eval_jaxpr/dot_general | solution.py:35
  303.4 2.9 copy.13
  306.3 0.0 reduce-scatter.2.cloned.1.call-update
  306.3 65.4 %reduce-scatter.2.cloned.1.call-done = f32[16,2048]{1,0:T(8,128)} async-done(((f32[256,2048]{1,0:T(8,128)}), f32[16,2048]{1,0:T(8,128)}) %reduce-scatter.2.cloned.1.call-update) | async-done | bytes 131088 | tf_op jit(solution)/shard_map/reduce_scatter | solution.py:39
  (5 shorter events, 0.0 us)
Async XLA Ops:
  38.7 219.4 %all-to-all-start.1 = ((bf16[1,1,32,128,256]{4,3,1,0,2:T(8,128)(2,1)}), bf16[1,1,32,128,256]{4,3,1,0,2:T(8,128)(2,1)}, u32[]{:S(2)}, u32[]{:S(2)}) async-start(bf16[1,1,32,128,256]{4,3,1,0,2:T(8,128)(2,1)} %bitcast.35), calls=%async_computation.1 | async-start | bytes 4194304 | tf_op jit(solution)/shard_map/all_to_all | solution.py:19
  44.6 188.5 %all-gather.2.cloned.1.call-start = ((), (), s32[]{:S(2)}) async-start(), calls=%async_computation.3 | async-start | bytes 3244032 | tf_op jit(solution)/shard_map/all_gather | solution.py:28
  45.3 326.5 %reduce-scatter.2.cloned.1.call-start = ((), (), s32[]{:S(2)}) async-start(), calls=%async_computation.4 | async-start | bytes 2228224 | tf_op jit(solution)/shard_map/reduce_scatter | solution.py:39
Sparse Core Ops, SparseCore 0:
  48.5 184.4 all-gather.1
  306.4 65.2 reduce-scatter.1
where the time goes:
time: 379 us
  waiting for transfers between devices  254 us (67%)
  matrix products  34.6 us (9%)
  blocking collectives  31.3 us (8%)
  local copies, waits for them, and re-layouts  31.2 us (8%)
  between operations  13.5 us (4%)
  other arithmetic  8.38 us (2%)
  starting transfers between devices  5.98 us (2%)
    all_gather x1, waiting for transfers between devices, per_device(): gathered = lax.all_gather(query_rows, 'blk', axis=0, tiled=True)  187 us
    reduce_scatter x1, waiting for transfers between devices, per_device(): lax.psum_scatter(partial_value, 'doc', scatter_dimension=0, tiled=True)  65.4 us
    dot_general x8, matrix products, block_tile(): return jnp.dot(picked_queries, masked, preferred_element_type=jnp.float32)  34.6 us
    all_to_all x1, blocking collectives, per_device(): lax.all_to_all(targets, 'blk', split_axis=2, concat_axis=2, tiled=True)  31.3 us
    gather x1, local copies, waits for them, and re-layouts, per_device(): picked_queries = jnp.take(gathered, safe_doc, axis=1)  16.9 us
  transfers between devices with their start and end apart: 3, of which 2 were waited for; matrix products, arithmetic and copies ran while one was open for 7% of the time, Pallas kernels for 0%

commit v1 on v0

--- a/solution.py
+++ b/solution.py
@@ -5,6 +5,11 @@
 
 F = 65536
 BW = 256
+
+
+def swapped_in(array, axis, dim):
+    sent = jnp.stack([array] * lax.axis_size(axis))
+    return jnp.concatenate(lax.all_to_all(sent, axis, 0, 0), axis=dim)
 
 
 def per_device(query_rows, row_values, row_slots, row_counts):
@@ -25,7 +30,7 @@
     doc_of = jnp.where(live_rows, flat_targets // per_owner, doc_count).astype(jnp.int32)
     block_of = flat_targets % per_owner
     block_ids = jnp.arange(per_owner, dtype=jnp.int32)
-    gathered = lax.all_gather(query_rows, "blk", axis=0, tiled=True)
+    gathered = swapped_in(query_rows, "blk", 0)
     safe_doc = jnp.minimum(doc_of, doc_count - 1)
     picked_queries = jnp.take(gathered, safe_doc, axis=1)
 

time: 379 us -> 411 us (1.084)
  blocking collectives: 31.3 us -> 181 us
  waiting for transfers between devices: 254 us -> 137 us
    all_gather x1 -> x0, waiting for transfers between devices: 187 us -> none  [per_device(): gathered = lax.all_gather(query_rows, 'blk', axis=0, tiled=True)]
    all_to_all x0 -> x1, blocking collectives: none -> 149 us  [swapped_in(): return jnp.concatenate(lax.all_to_all(sent, axis, 0, 0), axis=dim)]
    all_to_all x1, waiting for transfers between devices: 0.01 us -> 75.1 us  [per_device(): lax.all_to_all(row_values, 'blk', split_axis=2, concat_axis=2, tiled=True)]
  transfers between devices with their start and end apart: 3 -> 2, of which waited for: 2 -> 2; matrix products, arithmetic and copies ran while one was open for 7% -> 6% of each run, Pallas kernels for 0% -> 0%
where the time goes in v1:
time: 411 us
  blocking collectives  181 us (44%)
  waiting for transfers between devices  137 us (33%)
  matrix products  34.6 us (8%)
  local copies, waits for them, and re-layouts  32 us (8%)
  between operations  13.5 us (3%)
  other arithmetic  7.94 us (2%)
  starting transfers between devices  4.87 us (1%)
    all_to_all x1, blocking collectives, swapped_in(): return jnp.concatenate(lax.all_to_all(sent, axis, 0, 0), axis=dim)  149 us
    all_to_all x1, waiting for transfers between devices, per_device(): lax.all_to_all(row_values, 'blk', split_axis=2, concat_axis=2, tiled=True)  75.1 us
    reduce_scatter x1, waiting for transfers between devices, per_device(): lax.psum_scatter(partial_value, 'doc', scatter_dimension=0, tiled=True)  61.8 us
    dot_general x8, matrix products, block_tile(): return jnp.dot(picked_queries, masked, preferred_element_type=jnp.float32)  34.6 us
    all_to_all x1, blocking collectives, per_device(): lax.all_to_all(targets, 'blk', split_axis=2, concat_axis=2, tiled=True)  31.3 us
    gather x1, local copies, waits for them, and re-layouts, per_device(): picked_queries = jnp.take(gathered, safe_doc, axis=1)  17 us
  transfers between devices with their start and end apart: 2, of which 2 were waited for; matrix products, arithmetic and copies ran while one was open for 6% of the time, Pallas kernels for 0%

profile of v1, /device:TPU:32, one launch (start us, length us, event | category | flops | bytes accessed | tf_op | source)
XLA Modules:
  0.0 410.6 jit_solution(14481836137014315188)
XLA Ops:
  6.5 0.8 compare_select_fusion.2
  7.4 31.3 %all_to_all.15 = s32[1,1,32,128]{3,1,0,2:T(1,128)S(1)} all-to-all(s32[1,1,32,128]{3,1,0,2:T(1,128)S(1)} %compare_select_fusion.2), channel_id=1, replica_groups=mesh['doc'=16,'blk'=32] {'blk'}, dimensions={2} | all-to-all | bytes 32768 | tf_op jit(solution)/shard_map/all_to_all | solution.py:25
  38.7 1.2 stack.2
  39.9 149.4 %all_to_all.16 = bf16[32,8,6144]{2,1,0:T(8,128)(2,1)} all-to-all(bf16[32,8,6144]{2,1,0:T(8,128)(2,1)S(1)} %stack.2), channel_id=1, replica_groups=mesh['doc'=16,'blk'=32] {'blk'}, dimensions={0} | all-to-all | bytes 6291456 | tf_op jit(solution)/shard_map/all_to_all | solution.py:12
  189.3 4.8 %all-to-all-start.1 = ((bf16[1,1,32,128,256]{4,3,1,0,2:T(8,128)(2,1)}), bf16[1,1,32,128,256]{4,3,1,0,2:T(8,128)(2,1)}, u32[]{:S(2)}, u32[]{:S(2)}) async-start(bf16[1,1,32,128,256]{4,3,1,0,2:T(8,128)(2,1)} %bitcast.6), calls=%async_computation.1 | async-start | bytes 4194304 | tf_op jit(solution)/shard_map/all_to_all | solution.py:24
  194.1 0.0 reduce-scatter.2.cloned.1.call-start
  194.2 0.1 compare_select_fusion
  194.3 3.2 copy.13
  197.5 17.0 %gather_fusion = bf16[4096,256]{1,0:T(8,128)(2,1)} fusion(bf16[256,6144]{0,1:T(8,128)(2,1)S(1)} %copy.13, s32[4096]{0:T(1024)S(1)} %broadcast_clamp_fusion), kind=kCustom, calls=%fused_computation | custom fusion | bytes 4210688 | tf_op jit(solution)/shard_map/jit(_take)/gather | solution.py:35
  214.5 1.9 select_bitcast_fusion
  216.5 2.9 copy.14
  219.4 75.1 %all-to-all-done.1 = bf16[1,1,32,128,256]{4,3,1,0,2:T(8,128)(2,1)} async-done(((bf16[1,1,32,128,256]{4,3,1,0,2:T(8,128)(2,1)}), bf16[1,1,32,128,256]{4,3,1,0,2:T(8,128)(2,1)}, u32[]{:S(2)}, u32[]{:S(2)}) %all-to-all-start.1) | async-done | bytes 2097184 | tf_op jit(solution)/shard_map/all_to_all | solution.py:24
  294.5 44.5 %while.10 = (s32[]{:T(128)}, f32[8,256,256]{1,2,0:T(8,128)}, s32[8]{0:T(128)S(1)}, s32[4096]{0:T(1024)S(1)}, pred[4096]{0:T(1024)(128)(4,1)S(1)}, /*index=5*/bf1...) while((s32[]{:T(128)}, f32[8,256,256]{1,2,0:T(8,128)}, s32[8]{0:T(128)S(1)}, s32[4096]{0:T(1024)S(1)}, ...), condition=%wide.region_1.2_spmd, body=%wide.region_0.1_spmd.sunk | while | flops 537927680 | bytes 4485733 | solution.py:42
  294.5 0.6 dynamic_slice.5
  295.1 0.6 compare_and_fusion.3
  295.8 4.3 %fusion.21 = f32[8,256,256]{1,2,0:T(8,128)} fusion(f32[8,256,256]{1,2,0:T(8,128)} %get-tuple-element.132, s32[]{:T(128)} %get-tuple-element.131, bf16[256,4096]{1,0:T(8,128)(2,1)} %get-tuple-element.145, bf16[4096,256]{1,0:T(8,128)(2,1)} %get-tuple-element.144, pred[4096]{0:T(1024)(128)(4,1)S(1)} %compare_and_fusion.3), kind=kOutput, calls=%fused_computation.5.clone.1 | convolution fusion | flops 537919488 | bytes 4461056 | tf_op jit(solution)/shard_map/while/body/eval_jaxpr/dot_general | solution.py:40
  300.1 0.6 dynamic_slice.5
  300.7 0.6 compare_and_fusion.3
  301.3 4.3 %fusion.21 = f32[8,256,256]{1,2,0:T(8,128)} fusion(f32[8,256,256]{1,2,0:T(8,128)} %get-tuple-element.132, s32[]{:T(128)} %get-tuple-element.131, bf16[256,4096]{1,0:T(8,128)(2,1)} %get-tuple-element.145, bf16[4096,256]{1,0:T(8,128)(2,1)} %get-tuple-element.144, pred[4096]{0:T(1024)(128)(4,1)S(1)} %compare_and_fusion.3), kind=kOutput, calls=%fused_computation.5.clone.1 | convolution fusion | flops 537919488 | bytes 4461056 | tf_op jit(solution)/shard_map/while/body/eval_jaxpr/dot_general | solution.py:40
  305.6 0.6 dynamic_slice.5
  306.2 0.6 compare_and_fusion.3
  306.9 4.3 %fusion.21 = f32[8,256,256]{1,2,0:T(8,128)} fusion(f32[8,256,256]{1,2,0:T(8,128)} %get-tuple-element.132, s32[]{:T(128)} %get-tuple-element.131, bf16[256,4096]{1,0:T(8,128)(2,1)} %get-tuple-element.145, bf16[4096,256]{1,0:T(8,128)(2,1)} %get-tuple-element.144, pred[4096]{0:T(1024)(128)(4,1)S(1)} %compare_and_fusion.3), kind=kOutput, calls=%fused_computation.5.clone.1 | convolution fusion | flops 537919488 | bytes 4461056 | tf_op jit(solution)/shard_map/while/body/eval_jaxpr/dot_general | solution.py:40
  311.2 0.6 dynamic_slice.5
  311.8 0.6 compare_and_fusion.3
  312.4 4.3 %fusion.21 = f32[8,256,256]{1,2,0:T(8,128)} fusion(f32[8,256,256]{1,2,0:T(8,128)} %get-tuple-element.132, s32[]{:T(128)} %get-tuple-element.131, bf16[256,4096]{1,0:T(8,128)(2,1)} %get-tuple-element.145, bf16[4096,256]{1,0:T(8,128)(2,1)} %get-tuple-element.144, pred[4096]{0:T(1024)(128)(4,1)S(1)} %compare_and_fusion.3), kind=kOutput, calls=%fused_computation.5.clone.1 | convolution fusion | flops 537919488 | bytes 4461056 | tf_op jit(solution)/shard_map/while/body/eval_jaxpr/dot_general | solution.py:40
  316.7 0.6 dynamic_slice.5
  317.3 0.6 compare_and_fusion.3
  318.0 4.3 %fusion.21 = f32[8,256,256]{1,2,0:T(8,128)} fusion(f32[8,256,256]{1,2,0:T(8,128)} %get-tuple-element.132, s32[]{:T(128)} %get-tuple-element.131, bf16[256,4096]{1,0:T(8,128)(2,1)} %get-tuple-element.145, bf16[4096,256]{1,0:T(8,128)(2,1)} %get-tuple-element.144, pred[4096]{0:T(1024)(128)(4,1)S(1)} %compare_and_fusion.3), kind=kOutput, calls=%fused_computation.5.clone.1 | convolution fusion | flops 537919488 | bytes 4461056 | tf_op jit(solution)/shard_map/while/body/eval_jaxpr/dot_general | solution.py:40
  322.3 0.6 dynamic_slice.5
  322.9 0.6 compare_and_fusion.3
  323.5 4.3 %fusion.21 = f32[8,256,256]{1,2,0:T(8,128)} fusion(f32[8,256,256]{1,2,0:T(8,128)} %get-tuple-element.132, s32[]{:T(128)} %get-tuple-element.131, bf16[256,4096]{1,0:T(8,128)(2,1)} %get-tuple-element.145, bf16[4096,256]{1,0:T(8,128)(2,1)} %get-tuple-element.144, pred[4096]{0:T(1024)(128)(4,1)S(1)} %compare_and_fusion.3), kind=kOutput, calls=%fused_computation.5.clone.1 | convolution fusion | flops 537919488 | bytes 4461056 | tf_op jit(solution)/shard_map/while/body/eval_jaxpr/dot_general | solution.py:40
  327.9 0.6 dynamic_slice.5
  328.5 0.6 compare_and_fusion.3
  329.1 4.3 %fusion.21 = f32[8,256,256]{1,2,0:T(8,128)} fusion(f32[8,256,256]{1,2,0:T(8,128)} %get-tuple-element.132, s32[]{:T(128)} %get-tuple-element.131, bf16[256,4096]{1,0:T(8,128)(2,1)} %get-tuple-element.145, bf16[4096,256]{1,0:T(8,128)(2,1)} %get-tuple-element.144, pred[4096]{0:T(1024)(128)(4,1)S(1)} %compare_and_fusion.3), kind=kOutput, calls=%fused_computation.5.clone.1 | convolution fusion | flops 537919488 | bytes 4461056 | tf_op jit(solution)/shard_map/while/body/eval_jaxpr/dot_general | solution.py:40
  333.4 0.6 dynamic_slice.5
  334.0 0.6 compare_and_fusion.3
  334.7 4.3 %fusion.21 = f32[8,256,256]{1,2,0:T(8,128)} fusion(f32[8,256,256]{1,2,0:T(8,128)} %get-tuple-element.132, s32[]{:T(128)} %get-tuple-element.131, bf16[256,4096]{1,0:T(8,128)(2,1)} %get-tuple-element.145, bf16[4096,256]{1,0:T(8,128)(2,1)} %get-tuple-element.144, pred[4096]{0:T(1024)(128)(4,1)S(1)} %compare_and_fusion.3), kind=kOutput, calls=%fused_computation.5.clone.1 | convolution fusion | flops 537919488 | bytes 4461056 | tf_op jit(solution)/shard_map/while/body/eval_jaxpr/dot_general | solution.py:40
  339.0 2.9 copy.16
  341.9 0.0 reduce-scatter.2.cloned.1.call-update
  341.9 61.8 %reduce-scatter.2.cloned.1.call-done = f32[16,2048]{1,0:T(8,128)} async-done(((f32[256,2048]{1,0:T(8,128)}), f32[16,2048]{1,0:T(8,128)}) %reduce-scatter.2.cloned.1.call-update) | async-done | bytes 131088 | tf_op jit(solution)/shard_map/reduce_scatter | solution.py:44
  (5 shorter events, 0.0 us)
Async XLA Ops:
  189.3 105.3 %all-to-all-start.1 = ((bf16[1,1,32,128,256]{4,3,1,0,2:T(8,128)(2,1)}), bf16[1,1,32,128,256]{4,3,1,0,2:T(8,128)(2,1)}, u32[]{:S(2)}, u32[]{:S(2)}) async-start(bf16[1,1,32,128,256]{4,3,1,0,2:T(8,128)(2,1)} %bitcast.6), calls=%async_computation.1 | async-start | bytes 4194304 | tf_op jit(solution)/shard_map/all_to_all | solution.py:24
  194.1 209.7 %reduce-scatter.2.cloned.1.call-start = ((), (), s32[]{:S(2)}) async-start(), calls=%async_computation.4 | async-start | bytes 2228224 | tf_op jit(solution)/shard_map/reduce_scatter | solution.py:44
Sparse Core Ops, SparseCore 0:
  342.1 61.6 reduce-scatter.1
